TPU v7x, 32 devices: a whole 2x2x4 slice. The times are simulated.
32 devices in a mesh: ctx: 16 (over z, x, core), head: 2 (over y).
Axes of the slice: x: 2, y: 2, z: 4, core: 2. Of those that a mesh axis runs over, the one named last changes fastest.
Arguments:
- queries: bfloat16 [64, 2048], P(('ctx', 'head')), may hold values from -150 to 150
- new_block_keys: bfloat16 [64, 512], P(('ctx', 'head')), may hold values from -6 to 6
- new_block_values: bfloat16 [64, 512], P(('ctx', 'head')), may hold values from -6 to 6
- stored_keys: bfloat16 [7168, 512], P('ctx', 'head'), may hold values from -6 to 6
- stored_values: bfloat16 [7168, 512], P('ctx', 'head'), may hold values from -6 to 6
- stretch_start: int32 [1], replicated, may hold values from 3584 to 7168
- block_order: int32 [32], replicated, may hold values from 0 to 31, each once
Outputs:
- attended: bfloat16 [64, 2048], P(('ctx', 'head'))
Inputs may be any that keep to these rules, and one draw needn't show every extreme that they name: `block_order`: each value appears once.
All inputs are finite; a program needn't handle non-finite values.
Results may differ from a plain program's by a relative error of at most 0.0049.
Values may be sent and summed in bfloat16 or wider, within the bound.
A program may use at most 128 MiB of HBM per device.

v0:
```python
import math
import jax
import jax.numpy as jnp
from jax import lax
from jax.sharding import PartitionSpec as P

QUERY_HEADS = 16
KEY_VALUE_HEADS = 4
HEAD_WIDTH = 128
NEG_FILL = -1e30


def on_device(
    queries,
    new_block_keys,
    new_block_values,
    stored_keys,
    stored_values,
    stretch_start,
    block_order,
):
    local_query, local_keys, local_values = (
        lax.all_to_all(queries, "head", split_axis=1, concat_axis=0, tiled=True),
        lax.all_to_all(new_block_keys, "head", split_axis=1, concat_axis=0, tiled=True),
        lax.all_to_all(new_block_values, "head", split_axis=1, concat_axis=0, tiled=True),
    )
    query_rows = local_keys.shape[0]
    cache_rows = stored_keys.shape[0]
    kv_width = local_keys.shape[1]
    kv_heads = kv_width // HEAD_WIDTH
    query_group_width = QUERY_HEADS // KEY_VALUE_HEADS
    half_rows = query_rows // 2
    stretch_first = stretch_start[0]
    context = lax.axis_index("ctx")
    fresh_rows = context * query_rows + jnp.arange(query_rows, dtype=jnp.int32)
    fresh_pos = (
        stretch_first + block_order[fresh_rows // half_rows] * half_rows + fresh_rows % half_rows
    )
    cache_pos = context * cache_rows + jnp.arange(cache_rows, dtype=jnp.int32)
    key_pos = jnp.concatenate([fresh_pos, cache_pos])
    usable = jnp.concatenate([jnp.ones((query_rows,), dtype=bool), cache_pos < stretch_first])
    key_count = query_rows + cache_rows
    key_rows = jnp.concatenate([local_keys, stored_keys], axis=0).reshape(
        key_count, kv_heads, HEAD_WIDTH
    )
    value_rows = jnp.concatenate([local_values, stored_values], axis=0).reshape(
        key_count, kv_heads, HEAD_WIDTH
    )
    score_scale = 1.0 / math.sqrt(HEAD_WIDTH)
    piece = lax.all_gather(local_query, "ctx", axis=0, tiled=True)
    piece_rows = piece.shape[0]
    grouped = piece.reshape(piece_rows, kv_heads, query_group_width, HEAD_WIDTH)
    scores = (
        jnp.einsum("qhgd,khd->qhgk", grouped, key_rows, preferred_element_type=jnp.float32)
        * score_scale
    )
    row_index = jnp.arange(piece_rows, dtype=jnp.int32)
    query_pos = (
        stretch_first + block_order[row_index // half_rows] * half_rows + row_index % half_rows
    )
    allowed = usable[None, :] & (key_pos[None, :] <= query_pos[:, None])
    scores = jnp.where(allowed[:, None, None, :], scores, NEG_FILL)
    stretch_rows = scores.shape[0]
    peaks = lax.pmax(jnp.max(scores, axis=-1), "ctx")
    block_len = math.gcd(stretch_rows, 512)
    block_count = stretch_rows // block_len
    score_blocks = scores.reshape(block_count, block_len, kv_heads, query_group_width, key_count)
    peak_blocks = peaks.reshape(block_count, block_len, kv_heads, query_group_width)

    def weigh_block(inputs):
        block_scores, block_peaks = inputs
        weights = jnp.exp(block_scores - block_peaks[..., None])
        totals = jnp.sum(weights, axis=-1)
        product = jnp.einsum(
            "qhgk,khd->qhgd",
            weights.astype(jnp.bfloat16),
            value_rows,
            preferred_element_type=jnp.float32,
        )
        return (
            product.reshape(block_len, kv_heads * query_group_width * HEAD_WIDTH),
            totals.reshape(block_len, kv_heads * query_group_width),
        )

    sum_blocks, total_blocks = lax.map(weigh_block, (score_blocks, peak_blocks))
    weighted = sum_blocks.reshape(stretch_rows, kv_heads * query_group_width * HEAD_WIDTH)
    totals_all = total_blocks.reshape(stretch_rows, kv_heads * query_group_width)
    part_sums, part_totals = (
        lax.psum_scatter(weighted, "ctx", scatter_dimension=0, tiled=True),
        lax.psum_scatter(totals_all, "ctx", scatter_dimension=0, tiled=True),
    )
    own_rows = part_sums.shape[0]
    result = (
        part_sums.reshape(own_rows, kv_heads * query_group_width, HEAD_WIDTH)
        / part_totals[..., None]
    )
    result = result.reshape(own_rows, kv_heads * query_group_width * HEAD_WIDTH).astype(
        jnp.bfloat16
    )
    return lax.all_to_all(result, "head", split_axis=0, concat_axis=1, tiled=True)


def solution(mesh):
    return jax.shard_map(
        on_device,
        mesh=mesh,
        in_specs=(
            P(("ctx", "head"), None),
            P(("ctx", "head"), None),
            P(("ctx", "head"), None),
            P("ctx", "head"),
            P("ctx", "head"),
            P(),
            P(),
        ),
        out_specs=P(("ctx", "head"), None),
        check_vma=False,
    )
```

profile of v0, /device:TPU:0, one launch (start us, length us, event | category | flops | bytes accessed | tf_op | source)
XLA Modules:
  0.0 212.5 jit_solution(3873993751585935543)
XLA Ops:
  6.5 4.4 %all-to-all-start.1 = ((bf16[2,2,256]{2,0,1:T(2,128)(2,1)}), bf16[2,2,256]{2,0,1:T(2,128)(2,1)S(1)}, u32[]{:S(2)}, u32[]{:S(2)}) async-start(bf16[2,2,256]{2,0,1:T(2,128)(2,1)} %bitcast.60), calls=%async_computation.1 | async-start | bytes 4096 | tf_op jit(solution)/shard_map/all_to_all | solution.py:24
  11.6 0.6 copy-done.1
  12.3 0.6 gather_fusion
  12.9 0.8 gather_fusion.1
  13.7 0.9 copy-done.2
  14.7 3.3 %all-to-all-start = ((bf16[2,2,256]{2,0,1:T(2,128)(2,1)}), bf16[2,2,256]{2,0,1:T(2,128)(2,1)S(1)}, u32[]{:S(2)}, u32[]{:S(2)}) async-start(bf16[2,2,256]{2,0,1:T(2,128)(2,1)} %bitcast), calls=%async_computation | async-start | bytes 4096 | tf_op jit(solution)/shard_map/all_to_all | solution.py:25
  18.1 3.7 %all-to-all-done = bf16[2,2,256]{2,0,1:T(2,128)(2,1)S(1)} async-done(((bf16[2,2,256]{2,0,1:T(2,128)(2,1)}), bf16[2,2,256]{2,0,1:T(2,128)(2,1)S(1)}, u32[]{:S(2)}, u32[]{:S(2)}) %all-to-all-start) | async-done | bytes 2080 | tf_op jit(solution)/shard_map/all_to_all | solution.py:25
  21.8 3.2 %all-to-all-start.2 = ((bf16[2,2,1024]{2,0,1:T(2,128)(2,1)}), bf16[2,2,1024]{2,0,1:T(2,128)(2,1)S(1)}, u32[]{:S(2)}, u32[]{:S(2)}) async-start(bf16[2,2,1024]{2,0,1:T(2,128)(2,1)} %bitcast.11), calls=%async_computation.2 | async-start | bytes 16384 | tf_op jit(solution)/shard_map/all_to_all | solution.py:23
  25.1 0.1 compare_and_fusion
  25.2 0.6 copy-done.3
  25.9 0.6 dynamic-slice.2
  27.1 1.7 all-to-all-done.2
  28.9 22.4 %all-gather = bf16[16,4,1024]{2,1,0:T(4,128)(2,1)S(1)} all-gather(bf16[1,4,1024]{2,1,0:T(4,128)(2,1)S(1)} %reshape.221), channel_id=1, replica_groups=mesh['ctx'=16,'head'=2] {'ctx'}, dimensions={0}, use_global_device_ids=true | all-gather | bytes 139264 | tf_op jit(solution)/shard_map/all_gather | solution.py:50
  51.3 0.4 fusion.19
  51.7 29.8 %pmax.7 = f32[64,2,4]{0,2,1:T(4,128)S(1)} all-reduce(f32[64,2,4]{0,2,1:T(4,128)S(1)} %get-tuple-element.15), channel_id=1, replica_groups=mesh['ctx'=16,'head'=2] {'ctx'}, use_global_device_ids=true, to_apply=%region_1.2 | all-reduce | flops 512 | bytes 4096 | tf_op jit(solution)/shard_map/pmax | solution.py:64
  81.5 0.3 fusion.2
  81.9 29.5 %all-reduce.2 = f32[64,8]{0,1:T(8,128)S(1)} all-reduce(f32[64,8]{0,1:T(8,128)S(1)} %bitcast.57), channel_id=3, replica_groups=mesh['ctx'=16,'head'=2] {'ctx'}, use_global_device_ids=true, to_apply=%region_4.5.clone | all-reduce | flops 512 | bytes 4096
  111.5 0.4 convolution_bitcast_fusion
  111.9 0.2 copy.26
  112.1 0.8 reshape.203
  113.0 84.9 %all-reduce.5.cloned.1.call-done = f32[64,1024]{1,0:T(8,128)} async-done(((f32[64,1024]{1,0:T(8,128)}), f32[64,1024]{1,0:T(8,128)}) %all-reduce.5.cloned.1.call-update) | async-done | bytes 262160
  197.9 0.8 fusion.11
  198.7 6.4 %all_to_all.70 = bf16[2,2,1024]{2,1,0:T(2,128)(2,1)S(1)} all-to-all(bf16[2,2,1024]{2,1,0:T(2,128)(2,1)S(1)} %all_to_all.62), channel_id=1, replica_groups=mesh['ctx'=16,'head'=2] {'head'}, dimensions={0} | all-to-all | bytes 16384 | tf_op jit(solution)/shard_map/all_to_all | solution.py:100
  205.0 0.6 copy.47
  (30 shorter events, 0.7 us)
Async XLA Ops:
  6.5 7.1 %copy-start = (bf16[448,256]{1,0:T(8,128)(2,1)S(1)}, bf16[448,256]{1,0:T(8,128)(2,1)}, u32[]{:S(2)}) copy-start(bf16[448,256]{1,0:T(8,128)(2,1)} %param.10) | copy-start | bytes 688132
  6.5 8.2 %all-to-all-start.1 = ((bf16[2,2,256]{2,0,1:T(2,128)(2,1)}), bf16[2,2,256]{2,0,1:T(2,128)(2,1)S(1)}, u32[]{:S(2)}, u32[]{:S(2)}) async-start(bf16[2,2,256]{2,0,1:T(2,128)(2,1)} %bitcast.60), calls=%async_computation.1 | async-start | bytes 4096 | tf_op jit(solution)/shard_map/all_to_all | solution.py:24
  11.6 0.7 copy-start.1
  13.7 0.9 copy-start.2
  14.7 7.1 %all-to-all-start = ((bf16[2,2,256]{2,0,1:T(2,128)(2,1)}), bf16[2,2,256]{2,0,1:T(2,128)(2,1)S(1)}, u32[]{:S(2)}, u32[]{:S(2)}) async-start(bf16[2,2,256]{2,0,1:T(2,128)(2,1)} %bitcast), calls=%async_computation | async-start | bytes 4096 | tf_op jit(solution)/shard_map/all_to_all | solution.py:25
  21.8 7.0 %all-to-all-start.2 = ((bf16[2,2,1024]{2,0,1:T(2,128)(2,1)}), bf16[2,2,1024]{2,0,1:T(2,128)(2,1)S(1)}, u32[]{:S(2)}, u32[]{:S(2)}) async-start(bf16[2,2,1024]{2,0,1:T(2,128)(2,1)} %bitcast.11), calls=%async_computation.2 | async-start | bytes 16384 | tf_op jit(solution)/shard_map/all_to_all | solution.py:23
  25.1 172.8 %all-reduce.5.cloned.1.call-start = ((), (), s32[]{:S(2)}) async-start(), calls=%async_computation.4 | async-start | bytes 524288
  25.2 0.7 copy-start.3
Sparse Core Ops, SparseCore 0:
  113.0 84.7 all-reduce.4
where the time goes:
time: 213 us; the launch traced here: 212 us
  waiting for transfers between devices  90.3 us (42%)
  blocking collectives  88.1 us (41%)
  between operations  14.8 us (7%)
  starting transfers between devices  10.9 us (5%)
  local copies, waits for them, and re-layouts  6.24 us (3%)
    unnamed x2, waiting for transfers between devices  84.9 us
    pmax x1, blocking collectives, on_device(): peaks = lax.pmax(jnp.max(scores, axis=-1), 'ctx')  29.8 us
    unnamed x1, blocking collectives  29.5 us
    all_gather x1, blocking collectives, on_device(): piece = lax.all_gather(local_query, 'ctx', axis=0, tiled=True)  22.4 us
    all_to_all x1, blocking collectives, on_device(): lax.all_to_all(result, 'head', split_axis=0, concat_axis=1, tiled=True)  6.36 us
    all_to_all x1, starting transfers between devices, on_device(): lax.all_to_all(new_block_keys, 'head', split_axis=1, concat_axis=0, tiled...  4.37 us
  transfers between devices with their start and end apart: 4, of which 3 were waited for; matrix products, arithmetic and copies ran while one was open for 1% of the time, Pallas kernels for 0%

commit v1 on v0

--- a/solution.py
+++ b/solution.py
@@ -8,6 +8,27 @@
 KEY_VALUE_HEADS = 4
 HEAD_WIDTH = 128
 NEG_FILL = -1e30
+
+
+def ring_gather(array, axis, dim):
+    length, place, span = (lax.axis_size(axis), lax.axis_index(axis), array.shape[dim])
+    right = [(i, (i + 1) % length) for i in range(length)]
+    behind = [(i, (i - 1) % length) for i in range(length)]
+    out = jnp.zeros((*array.shape[:dim], length * span, *array.shape[dim + 1 :]), array.dtype)
+    out = lax.dynamic_update_slice_in_dim(out, array, place * span, axis=dim)
+    from_left = from_right = array
+    middle = length // 2
+    for hop in range(1, middle + 1):
+        from_left = lax.ppermute(from_left, axis, right)
+        out = lax.dynamic_update_slice_in_dim(
+            out, from_left, (place - hop) % length * span, axis=dim
+        )
+        if hop < length - middle:
+            from_right = lax.ppermute(from_right, axis, behind)
+            out = lax.dynamic_update_slice_in_dim(
+                out, from_right, (place + hop) % length * span, axis=dim
+            )
+    return out
 
 
 def on_device(
@@ -47,7 +68,7 @@
         key_count, kv_heads, HEAD_WIDTH
     )
     score_scale = 1.0 / math.sqrt(HEAD_WIDTH)
-    piece = lax.all_gather(local_query, "ctx", axis=0, tiled=True)
+    piece = ring_gather(local_query, "ctx", 0)
     piece_rows = piece.shape[0]
     grouped = piece.reshape(piece_rows, kv_heads, query_group_width, HEAD_WIDTH)
     scores = (

time: 213 us -> 236 us (1.11)
  starting transfers between devices: 10.9 us -> 41.8 us
  blocking collectives: 88.1 us -> 65.3 us
  waiting for transfers between devices: 90.3 us -> 106 us
    ppermute x0 -> x15, starting transfers between devices: none -> 30.9 us  [the longest x7 30.9 us: ring_gather(): from_right = lax.ppermute(from_right, axis, behind)]
    all_gather x1 -> x0, blocking collectives: 22.4 us -> none  [on_device(): piece = lax.all_gather(local_query, 'ctx', axis=0, tiled=True)]
    ppermute x0 -> x15, waiting for transfers between devices: none -> 15 us  [the longest x8 14.8 us: ring_gather(): from_left = lax.ppermute(from_left, axis, right)]
  transfers between devices with their start and end apart: 4 -> 19, of which waited for: 3 -> 12; matrix products, arithmetic and copies ran while one was open for 1% -> 1% of each run, Pallas kernels for 0% -> 0%
where the time goes in v1:
time: 236 us
  waiting for transfers between devices  106 us (45%)
  blocking collectives  65.3 us (28%)
  starting transfers between devices  41.8 us (18%)
  between operations  15.1 us (6%)
  local copies, waits for them, and re-layouts  5.11 us (2%)
    unnamed x2, waiting for transfers between devices  84.9 us
    ppermute x7, starting transfers between devices, ring_gather(): from_right = lax.ppermute(from_right, axis, behind)  30.9 us
    pmax x1, blocking collectives, on_device(): peaks = lax.pmax(jnp.max(scores, axis=-1), 'ctx')  29.5 us
    unnamed x1, blocking collectives  29.5 us
    ppermute x8, waiting for transfers between devices, ring_gather(): from_left = lax.ppermute(from_left, axis, right)  14.8 us
    all_to_all x1, blocking collectives, on_device(): lax.all_to_all(result, 'head', split_axis=0, concat_axis=1, tiled=True)  6.36 us
  transfers between devices with their start and end apart: 19, of which 12 were waited for; matrix products, arithmetic and copies ran while one was open for 1% of the time, Pallas kernels for 0%

profile of v1, /device:TPU:0, one launch (start us, length us, event | category | flops | bytes accessed | tf_op | source)
XLA Modules:
  0.0 235.8 jit_solution(1094296211128028852)
XLA Ops:
  6.5 4.4 %all-to-all-start.1 = ((bf16[2,2,256]{2,0,1:T(2,128)(2,1)}), bf16[2,2,256]{2,0,1:T(2,128)(2,1)S(1)}, u32[]{:S(2)}, u32[]{:S(2)}) async-start(bf16[2,2,256]{2,0,1:T(2,128)(2,1)} %bitcast.60), calls=%async_computation.1 | async-start | bytes 4096 | tf_op jit(solution)/shard_map/all_to_all | solution.py:45
  14.7 3.2 %all-to-all-start = ((bf16[2,2,256]{2,0,1:T(2,128)(2,1)}), bf16[2,2,256]{2,0,1:T(2,128)(2,1)S(1)}, u32[]{:S(2)}, u32[]{:S(2)}) async-start(bf16[2,2,256]{2,0,1:T(2,128)(2,1)} %bitcast), calls=%async_computation | async-start | bytes 4096 | tf_op jit(solution)/shard_map/all_to_all | solution.py:46
  17.9 3.7 %all-to-all-done = bf16[2,2,256]{2,0,1:T(2,128)(2,1)S(1)} async-done(((bf16[2,2,256]{2,0,1:T(2,128)(2,1)}), bf16[2,2,256]{2,0,1:T(2,128)(2,1)S(1)}, u32[]{:S(2)}, u32[]{:S(2)}) %all-to-all-start) | async-done | bytes 2080 | tf_op jit(solution)/shard_map/all_to_all | solution.py:46
  21.7 3.2 %all-to-all-start.2 = ((bf16[2,2,1024]{2,0,1:T(2,128)(2,1)}), bf16[2,2,1024]{2,0,1:T(2,128)(2,1)S(1)}, u32[]{:S(2)}, u32[]{:S(2)}) async-start(bf16[2,2,1024]{2,0,1:T(2,128)(2,1)} %bitcast.11), calls=%async_computation.2 | async-start | bytes 16384 | tf_op jit(solution)/shard_map/all_to_all | solution.py:44
  27.0 1.7 all-to-all-done.2
  28.7 4.4 %collective-permute-start.1 = (bf16[4,1024]{1,0:T(4,128)(2,1)S(1)}, bf16[4,1024]{1,0:T(4,128)(2,1)S(1)}, u32[]{:S(2)}, u32[]{:S(2)}) collective-permute-start(bf16[4,1024]{1,0:T(4,128)(2,1)S(1)} %all_to_all.61), channel_id=1, source_target_pairs={{0,30},{2,0},{4,2},{6,4},{8,6},{10,8},{12,10},{14,12},{16,14},{18,... | collective-permute-start | bytes 24584 | tf_op jit(solution)/shard_map/ppermute | solution.py:27
  33.2 1.3 collective-permute-done
  34.5 4.4 %collective-permute-start.3 = (bf16[4,1024]{1,0:T(4,128)(2,1)S(1)}, bf16[4,1024]{1,0:T(4,128)(2,1)S(1)}, u32[]{:S(2)}, u32[]{:S(2)}) collective-permute-start(bf16[4,1024]{1,0:T(4,128)(2,1)S(1)} %collective-permute-done.1), channel_id=1, source_target_pairs={{0,30},{2,0},{4,2},{6,4},{8,6},{10,8},{12,10},{14,12},{16,14},{18,... | collective-permute-start | bytes 24584 | tf_op jit(solution)/shard_map/ppermute | solution.py:27
  39.0 1.3 collective-permute-done.2
  40.3 4.4 %collective-permute-start.5 = (bf16[4,1024]{1,0:T(4,128)(2,1)S(1)}, bf16[4,1024]{1,0:T(4,128)(2,1)S(1)}, u32[]{:S(2)}, u32[]{:S(2)}) collective-permute-start(bf16[4,1024]{1,0:T(4,128)(2,1)S(1)} %collective-permute-done.3), channel_id=1, source_target_pairs={{0,30},{2,0},{4,2},{6,4},{8,6},{10,8},{12,10},{14,12},{16,14},{18,... | collective-permute-start | bytes 24584 | tf_op jit(solution)/shard_map/ppermute | solution.py:27
  44.7 1.3 collective-permute-done.4
  46.1 4.4 %collective-permute-start.7 = (bf16[4,1024]{1,0:T(4,128)(2,1)S(1)}, bf16[4,1024]{1,0:T(4,128)(2,1)S(1)}, u32[]{:S(2)}, u32[]{:S(2)}) collective-permute-start(bf16[4,1024]{1,0:T(4,128)(2,1)S(1)} %collective-permute-done.5), channel_id=1, source_target_pairs={{0,30},{2,0},{4,2},{6,4},{8,6},{10,8},{12,10},{14,12},{16,14},{18,... | collective-permute-start | bytes 24584 | tf_op jit(solution)/shard_map/ppermute | solution.py:27
  50.5 1.3 collective-permute-done.6
  51.9 4.4 %collective-permute-start.9 = (bf16[4,1024]{1,0:T(4,128)(2,1)S(1)}, bf16[4,1024]{1,0:T(4,128)(2,1)S(1)}, u32[]{:S(2)}, u32[]{:S(2)}) collective-permute-start(bf16[4,1024]{1,0:T(4,128)(2,1)S(1)} %collective-permute-done.7), channel_id=1, source_target_pairs={{0,30},{2,0},{4,2},{6,4},{8,6},{10,8},{12,10},{14,12},{16,14},{18,... | collective-permute-start | bytes 24584 | tf_op jit(solution)/shard_map/ppermute | solution.py:27
  56.3 1.3 collective-permute-done.8
  57.6 4.4 %collective-permute-start.11 = (bf16[4,1024]{1,0:T(4,128)(2,1)S(1)}, bf16[4,1024]{1,0:T(4,128)(2,1)S(1)}, u32[]{:S(2)}, u32[]{:S(2)}) collective-permute-start(bf16[4,1024]{1,0:T(4,128)(2,1)S(1)} %collective-permute-done.9), channel_id=1, source_target_pairs={{0,30},{2,0},{4,2},{6,4},{8,6},{10,8},{12,10},{14,12},{16,14},{18,... | collective-permute-start | bytes 24584 | tf_op jit(solution)/shard_map/ppermute | solution.py:27
  62.1 1.3 collective-permute-done.10
  63.4 4.4 %collective-permute-start.13 = (bf16[4,1024]{1,0:T(4,128)(2,1)S(1)}, bf16[4,1024]{1,0:T(4,128)(2,1)S(1)}, u32[]{:S(2)}, u32[]{:S(2)}) collective-permute-start(bf16[4,1024]{1,0:T(4,128)(2,1)S(1)} %collective-permute-done.11), channel_id=1, source_target_pairs={{0,30},{2,0},{4,2},{6,4},{8,6},{10,8},{12,10},{14,12},{16,14},{18,... | collective-permute-start | bytes 24584 | tf_op jit(solution)/shard_map/ppermute | solution.py:27
  67.8 1.3 collective-permute-done.12
  69.2 5.7 %collective-permute-done.14 = bf16[4,1024]{1,0:T(4,128)(2,1)S(1)} collective-permute-done((bf16[4,1024]{1,0:T(4,128)(2,1)S(1)}, bf16[4,1024]{1,0:T(4,128)(2,1)S(1)}, u32[]{:S(2)}, u32[]{:S(2)}) %collective-permute-start.14) | collective-permute-done | bytes 8224 | tf_op jit(solution)/shard_map/ppermute | solution.py:22
  75.4 29.5 %pmax.7 = f32[64,2,4]{0,2,1:T(4,128)S(1)} all-reduce(f32[64,2,4]{0,2,1:T(4,128)S(1)} %get-tuple-element.15), channel_id=1, replica_groups=mesh['ctx'=16,'head'=2] {'ctx'}, use_global_device_ids=true, to_apply=%region_1.2 | all-reduce | flops 512 | bytes 4096 | tf_op jit(solution)/shard_map/pmax | solution.py:85
  105.2 29.5 %all-reduce.2 = f32[64,8]{0,1:T(8,128)S(1)} all-reduce(f32[64,8]{0,1:T(8,128)S(1)} %bitcast.57), channel_id=3, replica_groups=mesh['ctx'=16,'head'=2] {'ctx'}, use_global_device_ids=true, to_apply=%region_4.5.clone | all-reduce | flops 512 | bytes 4096
  136.3 84.8 %all-reduce.5.cloned.1.call-done = f32[64,1024]{1,0:T(8,128)} async-done(((f32[64,1024]{1,0:T(8,128)}), f32[64,1024]{1,0:T(8,128)}) %all-reduce.5.cloned.1.call-update) | async-done | bytes 262160
  222.0 6.4 %all_to_all.70 = bf16[2,2,1024]{2,1,0:T(2,128)(2,1)S(1)} all-to-all(bf16[2,2,1024]{2,1,0:T(2,128)(2,1)S(1)} %all_to_all.62), channel_id=1, replica_groups=mesh['ctx'=16,'head'=2] {'head'}, dimensions={0} | all-to-all | bytes 16384 | tf_op jit(solution)/shard_map/all_to_all | solution.py:121
  (76 shorter events, 8.6 us)
Async XLA Ops:
  6.5 4.4 %copy-start = (bf16[448,256]{1,0:T(8,128)(2,1)S(1)}, bf16[448,256]{1,0:T(8,128)(2,1)}, u32[]{:S(2)}) copy-start(bf16[448,256]{1,0:T(8,128)(2,1)} %param.10) | copy-start | bytes 688132
  6.5 8.1 %all-to-all-start.1 = ((bf16[2,2,256]{2,0,1:T(2,128)(2,1)}), bf16[2,2,256]{2,0,1:T(2,128)(2,1)S(1)}, u32[]{:S(2)}, u32[]{:S(2)}) async-start(bf16[2,2,256]{2,0,1:T(2,128)(2,1)} %bitcast.60), calls=%async_computation.1 | async-start | bytes 4096 | tf_op jit(solution)/shard_map/all_to_all | solution.py:45
  11.0 0.7 copy-start.1
  12.3 0.9 copy-start.2
  14.7 7.0 %all-to-all-start = ((bf16[2,2,256]{2,0,1:T(2,128)(2,1)}), bf16[2,2,256]{2,0,1:T(2,128)(2,1)S(1)}, u32[]{:S(2)}, u32[]{:S(2)}) async-start(bf16[2,2,256]{2,0,1:T(2,128)(2,1)} %bitcast), calls=%async_computation | async-start | bytes 4096 | tf_op jit(solution)/shard_map/all_to_all | solution.py:46
  21.7 7.0 %all-to-all-start.2 = ((bf16[2,2,1024]{2,0,1:T(2,128)(2,1)}), bf16[2,2,1024]{2,0,1:T(2,128)(2,1)S(1)}, u32[]{:S(2)}, u32[]{:S(2)}) async-start(bf16[2,2,1024]{2,0,1:T(2,128)(2,1)} %bitcast.11), calls=%async_computation.2 | async-start | bytes 16384 | tf_op jit(solution)/shard_map/all_to_all | solution.py:44
  24.9 196.3 %all-reduce.5.cloned.1.call-start = ((), (), s32[]{:S(2)}) async-start(), calls=%async_computation.4 | async-start | bytes 524288
  25.1 0.7 copy-start.3
  28.7 5.8 %collective-permute-start = (bf16[4,1024]{1,0:T(4,128)(2,1)S(1)}, bf16[4,1024]{1,0:T(4,128)(2,1)S(1)}, u32[]{:S(2)}, u32[]{:S(2)}) collective-permute-start(bf16[4,1024]{1,0:T(4,128)(2,1)S(1)} %all_to_all.61), channel_id=1, source_target_pairs={{0,2},{2,4},{4,6},{6,8},{8,10},{10,12},{12,14},{14,16},{16,18},{18... | collective-permute-start | bytes 24584 | tf_op jit(solution)/shard_map/ppermute | solution.py:22
  28.7 5.8 %collective-permute-start.1 = (bf16[4,1024]{1,0:T(4,128)(2,1)S(1)}, bf16[4,1024]{1,0:T(4,128)(2,1)S(1)}, u32[]{:S(2)}, u32[]{:S(2)}) collective-permute-start(bf16[4,1024]{1,0:T(4,128)(2,1)S(1)} %all_to_all.61), channel_id=1, source_target_pairs={{0,30},{2,0},{4,2},{6,4},{8,6},{10,8},{12,10},{14,12},{16,14},{18,... | collective-permute-start | bytes 24584 | tf_op jit(solution)/shard_map/ppermute | solution.py:27
  34.5 5.8 %collective-permute-start.2 = (bf16[4,1024]{1,0:T(4,128)(2,1)S(1)}, bf16[4,1024]{1,0:T(4,128)(2,1)S(1)}, u32[]{:S(2)}, u32[]{:S(2)}) collective-permute-start(bf16[4,1024]{1,0:T(4,128)(2,1)S(1)} %collective-permute-done), channel_id=1, source_target_pairs={{0,2},{2,4},{4,6},{6,8},{8,10},{10,12},{12,14},{14,16},{16,18},{18... | collective-permute-start | bytes 24584 | tf_op jit(solution)/shard_map/ppermute | solution.py:22
  34.5 5.8 %collective-permute-start.3 = (bf16[4,1024]{1,0:T(4,128)(2,1)S(1)}, bf16[4,1024]{1,0:T(4,128)(2,1)S(1)}, u32[]{:S(2)}, u32[]{:S(2)}) collective-permute-start(bf16[4,1024]{1,0:T(4,128)(2,1)S(1)} %collective-permute-done.1), channel_id=1, source_target_pairs={{0,30},{2,0},{4,2},{6,4},{8,6},{10,8},{12,10},{14,12},{16,14},{18,... | collective-permute-start | bytes 24584 | tf_op jit(solution)/shard_map/ppermute | solution.py:27
  40.3 5.8 %collective-permute-start.4 = (bf16[4,1024]{1,0:T(4,128)(2,1)S(1)}, bf16[4,1024]{1,0:T(4,128)(2,1)S(1)}, u32[]{:S(2)}, u32[]{:S(2)}) collective-permute-start(bf16[4,1024]{1,0:T(4,128)(2,1)S(1)} %collective-permute-done.2), channel_id=1, source_target_pairs={{0,2},{2,4},{4,6},{6,8},{8,10},{10,12},{12,14},{14,16},{16,18},{18... | collective-permute-start | bytes 24584 | tf_op jit(solution)/shard_map/ppermute | solution.py:22
  40.3 5.8 %collective-permute-start.5 = (bf16[4,1024]{1,0:T(4,128)(2,1)S(1)}, bf16[4,1024]{1,0:T(4,128)(2,1)S(1)}, u32[]{:S(2)}, u32[]{:S(2)}) collective-permute-start(bf16[4,1024]{1,0:T(4,128)(2,1)S(1)} %collective-permute-done.3), channel_id=1, source_target_pairs={{0,30},{2,0},{4,2},{6,4},{8,6},{10,8},{12,10},{14,12},{16,14},{18,... | collective-permute-start | bytes 24584 | tf_op jit(solution)/shard_map/ppermute | solution.py:27
  46.0 5.8 %collective-permute-start.6 = (bf16[4,1024]{1,0:T(4,128)(2,1)S(1)}, bf16[4,1024]{1,0:T(4,128)(2,1)S(1)}, u32[]{:S(2)}, u32[]{:S(2)}) collective-permute-start(bf16[4,1024]{1,0:T(4,128)(2,1)S(1)} %collective-permute-done.4), channel_id=1, source_target_pairs={{0,2},{2,4},{4,6},{6,8},{8,10},{10,12},{12,14},{14,16},{16,18},{18... | collective-permute-start | bytes 24584 | tf_op jit(solution)/shard_map/ppermute | solution.py:22
  46.1 5.8 %collective-permute-start.7 = (bf16[4,1024]{1,0:T(4,128)(2,1)S(1)}, bf16[4,1024]{1,0:T(4,128)(2,1)S(1)}, u32[]{:S(2)}, u32[]{:S(2)}) collective-permute-start(bf16[4,1024]{1,0:T(4,128)(2,1)S(1)} %collective-permute-done.5), channel_id=1, source_target_pairs={{0,30},{2,0},{4,2},{6,4},{8,6},{10,8},{12,10},{14,12},{16,14},{18,... | collective-permute-start | bytes 24584 | tf_op jit(solution)/shard_map/ppermute | solution.py:27
  51.8 5.8 %collective-permute-start.8 = (bf16[4,1024]{1,0:T(4,128)(2,1)S(1)}, bf16[4,1024]{1,0:T(4,128)(2,1)S(1)}, u32[]{:S(2)}, u32[]{:S(2)}) collective-permute-start(bf16[4,1024]{1,0:T(4,128)(2,1)S(1)} %collective-permute-done.6), channel_id=1, source_target_pairs={{0,2},{2,4},{4,6},{6,8},{8,10},{10,12},{12,14},{14,16},{16,18},{18... | collective-permute-start | bytes 24584 | tf_op jit(solution)/shard_map/ppermute | solution.py:22
  51.9 5.8 %collective-permute-start.9 = (bf16[4,1024]{1,0:T(4,128)(2,1)S(1)}, bf16[4,1024]{1,0:T(4,128)(2,1)S(1)}, u32[]{:S(2)}, u32[]{:S(2)}) collective-permute-start(bf16[4,1024]{1,0:T(4,128)(2,1)S(1)} %collective-permute-done.7), channel_id=1, source_target_pairs={{0,30},{2,0},{4,2},{6,4},{8,6},{10,8},{12,10},{14,12},{16,14},{18,... | collective-permute-start | bytes 24584 | tf_op jit(solution)/shard_map/ppermute | solution.py:27
  57.6 5.8 %collective-permute-start.10 = (bf16[4,1024]{1,0:T(4,128)(2,1)S(1)}, bf16[4,1024]{1,0:T(4,128)(2,1)S(1)}, u32[]{:S(2)}, u32[]{:S(2)}) collective-permute-start(bf16[4,1024]{1,0:T(4,128)(2,1)S(1)} %collective-permute-done.8), channel_id=1, source_target_pairs={{0,2},{2,4},{4,6},{6,8},{8,10},{10,12},{12,14},{14,16},{16,18},{18... | collective-permute-start | bytes 24584 | tf_op jit(solution)/shard_map/ppermute | solution.py:22
  57.6 5.8 %collective-permute-start.11 = (bf16[4,1024]{1,0:T(4,128)(2,1)S(1)}, bf16[4,1024]{1,0:T(4,128)(2,1)S(1)}, u32[]{:S(2)}, u32[]{:S(2)}) collective-permute-start(bf16[4,1024]{1,0:T(4,128)(2,1)S(1)} %collective-permute-done.9), channel_id=1, source_target_pairs={{0,30},{2,0},{4,2},{6,4},{8,6},{10,8},{12,10},{14,12},{16,14},{18,... | collective-permute-start | bytes 24584 | tf_op jit(solution)/shard_map/ppermute | solution.py:27
  63.4 5.8 %collective-permute-start.12 = (bf16[4,1024]{1,0:T(4,128)(2,1)S(1)}, bf16[4,1024]{1,0:T(4,128)(2,1)S(1)}, u32[]{:S(2)}, u32[]{:S(2)}) collective-permute-start(bf16[4,1024]{1,0:T(4,128)(2,1)S(1)} %collective-permute-done.10), channel_id=1, source_target_pairs={{0,2},{2,4},{4,6},{6,8},{8,10},{10,12},{12,14},{14,16},{16,18},{18... | collective-permute-start | bytes 24584 | tf_op jit(solution)/shard_map/ppermute | solution.py:22
  63.4 5.8 %collective-permute-start.13 = (bf16[4,1024]{1,0:T(4,128)(2,1)S(1)}, bf16[4,1024]{1,0:T(4,128)(2,1)S(1)}, u32[]{:S(2)}, u32[]{:S(2)}) collective-permute-start(bf16[4,1024]{1,0:T(4,128)(2,1)S(1)} %collective-permute-done.11), channel_id=1, source_target_pairs={{0,30},{2,0},{4,2},{6,4},{8,6},{10,8},{12,10},{14,12},{16,14},{18,... | collective-permute-start | bytes 24584 | tf_op jit(solution)/shard_map/ppermute | solution.py:27
  69.1 5.8 %collective-permute-start.14 = (bf16[4,1024]{1,0:T(4,128)(2,1)S(1)}, bf16[4,1024]{1,0:T(4,128)(2,1)S(1)}, u32[]{:S(2)}, u32[]{:S(2)}) collective-permute-start(bf16[4,1024]{1,0:T(4,128)(2,1)S(1)} %collective-permute-done.12), channel_id=1, source_target_pairs={{0,2},{2,4},{4,6},{6,8},{8,10},{10,12},{12,14},{14,16},{16,18},{18... | collective-permute-start | bytes 24584 | tf_op jit(solution)/shard_map/ppermute | solution.py:22
Sparse Core Ops, SparseCore 0:
  136.4 84.7 all-reduce.4
